TPU v7x, 768 devices: a whole 4x8x12 slice. The times are simulated.
768 devices in a mesh: group: 2 (over core), face: 6 (over z_lo), tile: 64 (over y, x, z_hi).
Axes of the slice: x: 4, y: 8, z: 12 (z_hi: 2, z_lo: 6; z = z_hi * 6 + z_lo), core: 2. Of those that a mesh axis runs over, the one named last changes fastest.
Arguments:
- tracers: float32 [6, 128, 8, 16, 316], P('face', ('group', 'tile')), may hold values from -6 to 6
- wind_field: float32 [6, 128, 8, 16, 158], P('face', ('group', 'tile')), may hold values from -0.45 to 0.45
- face_links: int32 [6, 4, 3], replicated, may hold values from 0 to 5, as said below
- owner_map: int32 [6, 128, 128, 1], P('face', ('group', 'tile')), may hold values from 0 to 63; in each aligned block of 128 rows (0 to 127, 128 to 255, ..., all dimensions but the last counted through in order) at most 4 rows name the same one
- first_layer: bfloat16 [64, 632, 512], P('tile'), may hold values from -0.25 to 0.25
- middle_layer: bfloat16 [64, 512, 512], P('tile'), may hold values from -0.25 to 0.25
- last_layer: bfloat16 [64, 512, 316], P('tile'), may hold values from -0.25 to 0.25
Outputs:
- updated: float32 [6, 128, 8, 16, 316], P('face', ('group', 'tile'))
Inputs may be any that keep to these rules, and one draw needn't show every extreme that they name: `face_links`: the table describes the edges of a cube: [f, e] gives the face across edge e of face f (e: 0 west, 1 east, 2 south, 3 north), the edge of that face on the shared boundary, and 1 if positions along the boundary run in opposite directions on the two faces, else 0. For some f, faces f and (f + 3) % 6 share an edge where the west edge of one meets the east edge of the other with positions running the same way. `owner_map`: among the 128 columns of one block of one face, no owner is named by more than 4 columns.
All inputs are finite; a program needn't handle non-finite values.
Results may differ from a plain program's by a relative error of at most 0.0016.
Values may be sent and summed in bfloat16 or wider, within the bound.
A program may use at most 32 MiB of HBM per device.

v0:
```python
import jax
import jax.numpy as jnp
from jax import lax
from jax.sharding import PartitionSpec as P

ACROSS = 8


def from_behind(value, axis, steps):
    count = lax.axis_size(axis)
    pairs = [(source, (source + steps) % count) for source in range(count)]
    return lax.ppermute(value, axis, pairs)


def split_flow(values, speed):
    levels = speed.shape[-1]
    shaped = values.reshape(values.shape[:-1] + (4, levels))
    forward = (shaped * jnp.maximum(speed, 0.0)[..., None, :]).reshape(values.shape)
    backward = (shaped * jnp.minimum(speed, 0.0)[..., None, :]).reshape(values.shape)
    return (forward, backward)


def inflow_term(values, outward):
    levels = outward.shape[-1]
    shaped = values.reshape(values.shape[:-1] + (4, levels))
    return (shaped * jnp.maximum(outward, 0.0)[..., None, :]).reshape(values.shape)


def edge_payload(values, outward):
    return jnp.concatenate([values, outward], axis=-1)


def payload_inflow(payload, levels):
    return inflow_term(payload[..., : 4 * levels], payload[..., 4 * levels :])


def from_block(strip, offset):
    return from_behind(strip, ("group", "tile"), offset)


def local(tracers, wind_field, face_links, owner_map, first_layer, middle_layer, last_layer):
    fields = tracers[:, 0]
    winds = wind_field[:, 0]
    face_count, row_count, col_count, field_width = fields.shape
    levels = field_width // 4
    u_wind = winds[..., :levels]
    v_wind = winds[..., levels:]
    tile_count = lax.axis_size("tile")
    half_cols = ACROSS // 2
    block_rows = tile_count // half_cols
    face_side = ACROSS * col_count
    group_now = lax.axis_index("group")
    tile_now = lax.axis_index("tile")
    block_row = tile_now // half_cols
    within = tile_now % half_cols
    lower = group_now == 0
    block_col = jnp.where(lower, within, ACROSS - 1 - within)
    face_dev = lax.axis_index("face")
    face_devices = lax.axis_size("face")
    west_edge = edge_payload(fields[:, :, 0], -u_wind[:, :, 0])
    east_edge = edge_payload(fields[:, :, -1], u_wind[:, :, -1])
    south_edge = edge_payload(fields[:, 0], -v_wind[:, 0])
    north_edge = edge_payload(fields[:, -1], v_wind[:, -1])
    payload_width = west_edge.shape[-1]
    toward_far = jnp.where(lower, east_edge, west_edge)
    toward_near = jnp.where(lower, west_edge, east_edge)
    from_before = from_block(toward_far, 1)
    from_after = from_block(toward_near, -1)
    from_other = from_block(toward_far, tile_count)
    middle = within == half_cols - 1
    west_beside = jnp.where(lower, from_before, jnp.where(middle, from_other, from_after))
    east_beside = jnp.where(lower, jnp.where(middle, from_other, from_after), from_before)
    south_beside = from_block(north_edge, half_cols)
    north_beside = from_block(south_edge, -half_cols)
    beside = [west_beside, east_beside, south_beside, north_beside]
    on_edge = [block_col == 0, block_col == ACROSS - 1, block_row == 0, block_row == block_rows - 1]
    starts = [
        block_row * row_count,
        block_row * row_count,
        block_col * col_count,
        block_col * col_count,
    ]
    lengths = [row_count, row_count, col_count, col_count]
    strips = [west_edge, east_edge, south_edge, north_edge]
    slot_rows = max(row_count, col_count)
    face_rim = jnp.zeros((face_count, 4 * face_side, payload_width), jnp.float32)
    for edge_id in range(4):
        placed = jnp.where(on_edge[edge_id], strips[edge_id], 0.0)
        face_rim = lax.dynamic_update_slice(
            face_rim, placed, (jnp.int32(0), edge_id * face_side + starts[edge_id], jnp.int32(0))
        )
    face_rim = lax.psum(face_rim, ("group", "tile"))
    outgoing = []
    for target_dev in range(face_devices):
        local_face = 0
        target_face = target_dev * face_count + local_face
        source_face = face_dev * face_count + 0
        strip_out = jnp.zeros((slot_rows, payload_width), jnp.float32)
        for edge_id in range(4):
            link_row = face_links[target_face, edge_id]
            span_rows = lengths[edge_id]
            reverse_run = link_row[2] == 1
            start_at = jnp.where(
                reverse_run, face_side - starts[edge_id] - span_rows, starts[edge_id]
            )
            offset = link_row[1] * face_side + start_at
            matched = jnp.logical_and(link_row[0] == source_face, on_edge[edge_id])
            sliced = lax.dynamic_slice(
                face_rim, (jnp.int32(0), offset, jnp.int32(0)), (1, span_rows, payload_width)
            )[0]
            sliced = jnp.where(reverse_run, sliced[::-1], sliced)
            sliced = jnp.pad(sliced, ((0, slot_rows - span_rows), (0, 0)))
            strip_out = jnp.where(matched, sliced, strip_out)
        for_face = [strip_out]
        for_device = [jnp.stack(for_face)]
        outgoing.append(jnp.stack(for_device))
    incoming = lax.all_to_all(
        jnp.stack(outgoing).astype(jnp.bfloat16), "face", split_axis=0, concat_axis=0, tiled=True
    ).astype(jnp.float32)
    across_edges = []
    for edge_id in range(4):
        local_face = 0
        face_id = face_dev * face_count + local_face
        neighbour = face_links[face_id, edge_id][0]
        received = incoming[neighbour // face_count, local_face, neighbour % face_count]
        across_faces = [received[: lengths[edge_id]]]
        across_edges.append(jnp.stack(across_faces))
    inflows = []
    for edge_id in range(4):
        chosen = jnp.where(on_edge[edge_id], across_edges[edge_id], beside[edge_id])
        inflows.append(payload_inflow(chosen, levels))
    east_flow, west_flow = split_flow(fields, u_wind)
    north_flow, south_flow = split_flow(fields, v_wind)
    flux_x = jnp.concatenate([inflows[0][:, :, None], east_flow], axis=2) + jnp.concatenate(
        [west_flow, -inflows[1][:, :, None]], axis=2
    )
    flux_y = jnp.concatenate([inflows[2][:, None], north_flow], axis=1) + jnp.concatenate(
        [south_flow, -inflows[3][:, None]], axis=1
    )
    advected = fields - (flux_x[:, :, 1:] - flux_x[:, :, :-1]) - (flux_y[:, 1:] - flux_y[:, :-1])
    cell_count = row_count * col_count
    inputs = jnp.concatenate(
        [advected.astype(jnp.bfloat16), (advected - fields).astype(jnp.bfloat16)], axis=-1
    )
    inputs = inputs.reshape(face_count * cell_count, 8 * levels)
    routes = owner_map[:, 0, :, 0]
    capacity = 2 * cell_count // tile_count
    picked = (routes[..., None] == jnp.arange(tile_count, dtype=jnp.int32)).astype(jnp.int32)
    ranking = jnp.sum(picked * (jnp.cumsum(picked, axis=1) - 1), axis=-1)
    per_owner = face_count * capacity
    slot_ids = (
        routes * per_owner + jnp.arange(face_count, dtype=jnp.int32)[:, None] * capacity + ranking
    )
    slot_ids = slot_ids.reshape(-1)
    sources = (
        jnp.zeros((tile_count * per_owner,), jnp.int32)
        .at[slot_ids]
        .set(jnp.arange(face_count * cell_count, dtype=jnp.int32) + 1)
    )
    outgoing_cols = jnp.where(
        (sources > 0)[:, None], inputs[jnp.maximum(sources - 1, 0)], jnp.zeros((), jnp.bfloat16)
    )
    outgoing_cols = outgoing_cols.reshape(tile_count, per_owner, 8 * levels)
    arrived = lax.all_to_all(outgoing_cols, "tile", split_axis=0, concat_axis=0, tiled=True)
    columns = arrived.reshape(-1, arrived.shape[-1])
    hidden_one = jax.nn.silu(
        jnp.dot(columns, first_layer[0], preferred_element_type=jnp.float32)
    ).astype(jnp.bfloat16)
    hidden_two = jax.nn.silu(
        jnp.dot(hidden_one, middle_layer[0], preferred_element_type=jnp.float32)
    ).astype(jnp.bfloat16)
    tendency = jnp.dot(hidden_two, last_layer[0], preferred_element_type=jnp.float32).astype(
        jnp.bfloat16
    )
    tendency = tendency.reshape(arrived.shape[:-1] + (tendency.shape[-1],))
    returned = lax.all_to_all(tendency, "tile", split_axis=0, concat_axis=0, tiled=True)
    tendency = returned.reshape(-1, 4 * levels)[slot_ids].reshape(
        face_count, row_count, col_count, 4 * levels
    )
    updated = advected + tendency.astype(jnp.float32)
    return updated[:, None]


def solution(mesh):
    in_specs = (
        P("face", ("group", "tile"), None, None, None),
        P("face", ("group", "tile"), None, None, None),
        P(),
        P("face", ("group", "tile"), None, None),
        P("tile", None, None),
        P("tile", None, None),
        P("tile", None, None),
    )
    out_specs = P("face", ("group", "tile"), None, None, None)
    return jax.shard_map(local, mesh=mesh, in_specs=in_specs, out_specs=out_specs, check_vma=False)
```

profile of v0, /device:TPU:6, one launch (start us, length us, event | category | flops | bytes accessed | tf_op | source)
XLA Modules:
  0.0 1190.7 jit_solution(3005244734575022696)
XLA Ops:
  0.0 1.1 copy.73
  1.4 15.1 %collective-permute-start = (f32[1,8,395]{2,1,0:T(8,128)S(1)}, f32[1,8,395]{2,1,0:T(8,128)S(1)}, u32[]{:S(2)}, u32[]{:S(2)}) collective-permute-start(f32[1,8,395]{2,1,0:T(8,128)S(1)} %get-tuple-element.56), channel_id=1, source_target_pairs={{0,1},{1,2},{2,3},{3,4},{4,5},{5,6},{6,7},{7,8},{8,9},{9,10},{10,1... | collective-permute-start | bytes 37928 | tf_op jit(solution)/shard_map/ppermute | solution.py:12
  16.5 1.9 collective-permute-start.1
  18.6 0.7 copy-done.2
  19.3 0.7 constant_dynamic-slice_fusion.4
  24.9 0.7 fusion.55
  30.6 0.7 fusion.54
  33.9 0.7 fusion.56
  52.4 981.9 %all-reduce.13 = bf16[1,512,395]{2,1,0:T(8,128)(2,1)S(1)} all-reduce(f32[1,512,395]{2,1,0:T(8,128)S(1)} %copy_dynamic-update-slice_fusion), channel_id=1, replica_groups=mesh['group'=2,'face'=6,'tile'=64] {'group','tile'}, use_global_device_ids=true, to_apply=%region_0.1 | all-reduce | flops 202240 | bytes 1213440 | tf_op jit(solution)/shard_map/psum | solution.py:92
  1052.5 0.6 fusion.24
  1053.1 0.6 fusion.26
  1056.2 9.0 all-to-all-start
  1065.2 3.2 collective-permute-start.2
  1068.4 1.9 collective-permute-start.4
  1070.3 11.7 collective-permute-start.3
  1083.1 0.6 copy-done.3
  1084.2 1.0 scatter_custom_fusion
  1094.8 1.2 gather_fusion
  1096.4 65.5 %all_to_all.15 = bf16[64,4,632]{2,1,0:T(4,128)(2,1)S(1)} all-to-all(bf16[64,4,632]{2,1,0:T(4,128)(2,1)S(1)} %broadcast_select_fusion), channel_id=1, replica_groups=mesh['group'=2,'face'=6,'tile'=64] {'tile'}, dimensions={0} | all-to-all | bytes 647168 | tf_op jit(solution)/shard_map/all_to_all | solution.py:164
  1164.0 0.7 reshape.1105
  1164.7 8.7 all-to-all-start.2
  1173.5 15.4 %all-to-all-done.2 = bf16[64,4,316]{2,1,0:T(4,128)(2,1)S(1)} async-done(((bf16[64,4,316]{2,1,0:T(4,128)(2,1)}), bf16[64,4,316]{2,1,0:T(4,128)(2,1)S(1)}, u32[]{:S(2)}, u32[]{:S(2)}) %all-to-all-start.2) | async-done | bytes 161824 | tf_op jit(solution)/shard_map/all_to_all | solution.py:176
  1189.0 0.9 gather_fusion.1
  1190.0 0.7 copy.53
  (120 shorter events, 11.5 us)
Async XLA Ops:
  0.0 1162.1 %copy-start = (bf16[1,632,512]{2,1,0:T(8,128)(2,1)S(1)}, bf16[1,632,512]{2,1,0:T(8,128)(2,1)}, u32[]{:S(2)}) copy-start(bf16[1,632,512]{2,1,0:T(8,128)(2,1)} %param.11) | copy-start | bytes 1941508
  0.0 1.1 copy-start.1
  1.4 1092.0 %collective-permute-start = (f32[1,8,395]{2,1,0:T(8,128)S(1)}, f32[1,8,395]{2,1,0:T(8,128)S(1)}, u32[]{:S(2)}, u32[]{:S(2)}) collective-permute-start(f32[1,8,395]{2,1,0:T(8,128)S(1)} %get-tuple-element.56), channel_id=1, source_target_pairs={{0,1},{1,2},{2,3},{3,4},{4,5},{5,6},{6,7},{7,8},{8,9},{9,10},{10,1... | collective-permute-start | bytes 37928 | tf_op jit(solution)/shard_map/ppermute | solution.py:12
  16.5 1076.8 %collective-permute-start.1 = (f32[1,8,395]{2,1,0:T(8,128)S(1)}, f32[1,8,395]{2,1,0:T(8,128)S(1)}, u32[]{:S(2)}, u32[]{:S(2)}) collective-permute-start(f32[1,8,395]{2,1,0:T(8,128)S(1)} %get-tuple-element.56), channel_id=1, source_target_pairs={{0,384},{1,385},{2,386},{3,387},{4,388},{5,389},{6,390},{7,391},{8... | collective-permute-start | bytes 37928 | tf_op jit(solution)/shard_map/ppermute | solution.py:12
  18.6 0.7 copy-start.2
  1056.2 37.1 %all-to-all-start = ((bf16[6,1,1,16,395]{4,3,2,1,0:T(8,128)(2,1)}), bf16[6,1,1,16,395]{4,3,2,1,0:T(8,128)(2,1)S(1)}, u32[]{:S(2)}, u32[]{:S(2)}) async-start(bf16[6,1,1,16,395]{4,3,2,1,0:T(8,128)(2,1)} %fusion.34), calls=%async_computation | async-start | bytes 196608 | tf_op jit(solution)/shard_map/all_to_all | solution.py:117
  1065.2 28.2 %collective-permute-start.2 = (f32[1,8,395]{2,1,0:T(8,128)S(1)}, f32[1,8,395]{2,1,0:T(8,128)S(1)}, u32[]{:S(2)}, u32[]{:S(2)}) collective-permute-start(f32[1,8,395]{2,1,0:T(8,128)S(1)} %get-tuple-element.55), channel_id=1, source_target_pairs={{0,447},{1,0},{2,1},{3,2},{4,3},{5,4},{6,5},{7,6},{8,7},{9,8},{10,... | collective-permute-start | bytes 37928 | tf_op jit(solution)/shard_map/ppermute | solution.py:12
  1068.4 25.3 %collective-permute-start.4 = (f32[1,16,395]{2,0,1:T(1,128)S(1)}, f32[1,16,395]{2,0,1:T(1,128)S(1)}, u32[]{:S(2)}, u32[]{:S(2)}) collective-permute-start(f32[1,16,395]{2,0,1:T(1,128)S(1)} %get-tuple-element.10), channel_id=1, source_target_pairs={{0,444},{1,445},{2,446},{3,447},{4,0},{5,1},{6,2},{7,3},{8,4},{9,5... | collective-permute-start | bytes 75848 | tf_op jit(solution)/shard_map/ppermute | solution.py:12
  1070.3 23.7 %collective-permute-start.3 = (f32[1,16,395]{2,0,1:T(1,128)S(1)}, f32[1,16,395]{2,0,1:T(1,128)S(1)}, u32[]{:S(2)}, u32[]{:S(2)}) collective-permute-start(f32[1,16,395]{2,0,1:T(1,128)S(1)} %get-tuple-element.8), channel_id=1, source_target_pairs={{0,4},{1,5},{2,6},{3,7},{4,8},{5,9},{6,10},{7,11},{8,12},{9,13},{1... | collective-permute-start | bytes 75848 | tf_op jit(solution)/shard_map/ppermute | solution.py:12
  1083.1 0.7 copy-start.3
  1162.1 1.0 copy-start.4
  1162.1 1.1 copy-start.5
  1164.7 24.2 %all-to-all-start.2 = ((bf16[64,4,316]{2,1,0:T(4,128)(2,1)}), bf16[64,4,316]{2,1,0:T(4,128)(2,1)S(1)}, u32[]{:S(2)}, u32[]{:S(2)}) async-start(bf16[64,4,316]{2,1,0:T(4,128)(2,1)} %reshape.1105), calls=%async_computation.2 | async-start | bytes 393216 | tf_op jit(solution)/shard_map/all_to_all | solution.py:176
where the time goes:
time: 1190 us
  blocking collectives  1050 us (88%)
  between operations  53.7 us (5%)
  starting transfers between devices  51.5 us (4%)
  local copies, waits for them, and re-layouts  15.4 us (1%)
  waiting for transfers between devices  15.4 us (1%)
    psum x1, blocking collectives, local(): face_rim = lax.psum(face_rim, ('group', 'tile'))  982 us
    all_to_all x1, blocking collectives, local(): lax.all_to_all(outgoing_cols, 'tile', split_axis=0, concat_axis=0, tiled=...  65.5 us
    ppermute x5, starting transfers between devices, from_behind(): return lax.ppermute(value, axis, pairs)  33.8 us
  transfers between devices with their start and end apart: 7, of which 1 were waited for; matrix products, arithmetic and copies ran while one was open for 1% of the time, Pallas kernels for 0%

commit v1 on v0

v1 whole, which is shorter than its diff:
```python
import functools

import jax
import jax.numpy as jnp
from jax import lax
from jax.experimental import pallas as pl
from jax.experimental.pallas import tpu as pltpu
from jax.sharding import PartitionSpec as P

MESH = pl.DeviceIdType.MESH
ROWS, COLS, LEV = 8, 16, 79
CELLS = ROWS * COLS
WIDE = 4 * LEV
PAD = 384
FEAT = 2 * WIDE
FPAD = 640
TILES = 64
CAP = 4
SLOTS = TILES * CAP
F32, BF16, I32 = jnp.float32, jnp.bfloat16, jnp.int32


def iota(shape, dim):
    return lax.broadcasted_iota(I32, shape, dim)


def onehot(condition):
    return jnp.where(condition, 1.0, 0.0).astype(BF16)


def silu(x):
    return x / (1.0 + jnp.exp(-x))


def dot(a, b):
    return jnp.dot(a, b, preferred_element_type=F32)


def place_of(col):
    lower = col < 4
    return jnp.where(lower, 0, 1), jnp.where(lower, col, 7 - col)


def kernel(
    q_ref, w_ref, links, owner_ref, first_hbm, middle_hbm, last_hbm,
    out_ref,
    first, middle, last,
    strip_v, strip_h, ghost_v, ghost_h,
    cand_v, cand_h, fwd_v, fwd_h, rim_v, rim_h,
    wide, outbox, inbox, reply, answers,
    wsem, halo_send, halo_recv, cand_send, cand_recv, rim_send_v, rim_send_h, rim_recv,
    a2a_send, a2a_recv, ret_send, ret_recv, own_sem,
):
    group, face, tile = (lax.axis_index(a) for a in ("group", "face", "tile"))
    row = tile // 4
    within = tile % 4
    col = jnp.where(group == 0, within, 7 - within)
    is_v = within == 0
    is_n = row == 15
    is_h = jnp.logical_or(row == 0, is_n)
    edge_v = group
    edge_h = jnp.where(is_n, 1, 0)

    loads = [
        pltpu.make_async_copy(first_hbm, first, wsem.at[0]),
        pltpu.make_async_copy(middle_hbm, middle, wsem.at[1]),
        pltpu.make_async_copy(last_hbm, last, wsem.at[2]),
    ]
    for load in loads:
        load.start()

    def device(r, c):
        g, k = place_of(c)
        return (g, face, r * 4 + k)

    halo = [
        (col > 0, device(row, col - 1), strip_v.at[0], ghost_v.at[1], halo_send.at[0], halo_recv.at[1]),
        (col < 7, device(row, col + 1), strip_v.at[1], ghost_v.at[0], halo_send.at[1], halo_recv.at[0]),
        (row > 0, device(row - 1, col), strip_h.at[0], ghost_h.at[1], halo_send.at[2], halo_recv.at[3]),
        (row < 15, device(row + 1, col), strip_h.at[1], ghost_h.at[0], halo_send.at[3], halo_recv.at[2]),
    ]
    relay = []

    def to_relay(role, r, c, source, target, which):
        n = len(relay)
        relay.append((role, r, c, source, target, cand_send.at[n], cand_recv.at[which]))

    mine_v = strip_v.at[edge_v]
    mine_h = strip_h.at[edge_h]
    for far in (0, 1):
        for rev in (0, 1):
            r = 15 - row if rev else row
            c = 7 - col if far else col
            to_relay(is_v, r, c, mine_v, cand_v.at[edge_v * 2 + rev], 0)
    for r in (0, 15):
        for rev in (0, 1):
            c = row // 2
            c = 7 - c if rev else c
            to_relay(is_v, jnp.int32(r), c, mine_v, cand_h.at[edge_v * 2 + rev, row % 2], 1)
    for far in (0, 1):
        for rev in (0, 1):
            r = 15 - row if far else row
            c = 7 - col if rev else col
            to_relay(is_h, r, c, mine_h, cand_h.at[4 + edge_h * 2 + rev], 1)
    for c in (0, 7):
        for rev in (0, 1):
            for b in (0, 1):
                r = 2 * col + b
                r = 15 - r if rev else r
                to_relay(is_h, r, jnp.int32(c), mine_h.at[b], cand_v.at[4 + edge_h * 2 + rev], 0)

    def elsewhere(r, c):
        return jnp.logical_or(r != row, c != col)

    def face_at(step):
        return lax.rem(face + step, 6)

    barrier = pltpu.get_barrier_semaphore()

    def signal(dev):
        pl.semaphore_signal(barrier, inc=1, device_id=dev, device_id_type=MESH)

    def count(condition):
        return jnp.where(condition, 1, 0)

    arrivals = jnp.int32(TILES - 1)
    for condition, dev, *_ in halo:
        pl.when(condition)(functools.partial(signal, dev))
        arrivals += count(condition)
    for role, r, c, *_ in relay:
        condition = jnp.logical_and(role, elsewhere(r, c))
        pl.when(condition)(functools.partial(signal, device(r, c)))
        arrivals += count(condition)
    for role in (is_v, is_h):
        @pl.when(role)
        def _():
            for step in range(1, 6):
                signal((group, face_at(step), tile))
        arrivals += 5 * count(role)

    def owner_at(i):
        y = lax.rem(tile // 8 + i // 8, 8)
        x = lax.rem((tile // 2) % 4 + (i // 2) % 4, 4)
        z = lax.rem(tile % 2 + i % 2, 2)
        return y * 8 + x * 2 + z

    def signal_owner(i, carry):
        signal((group, face, owner_at(i)))
        return carry

    lax.fori_loop(1, TILES, signal_owner, 0)

    wide[:, 256:] = jnp.zeros((CELLS, PAD - 256), F32)
    wide[:, :WIDE] = q_ref[...]
    q = wide[...]
    winds = w_ref[...]
    level = lax.rem(iota((2 * LEV, PAD), 1), LEV)
    inside = iota((2 * LEV, PAD), 1) < WIDE
    spread_u = jnp.where(jnp.logical_and(inside, iota((2 * LEV, PAD), 0) == level), 1.0, 0.0)
    spread_v = jnp.where(jnp.logical_and(inside, iota((2 * LEV, PAD), 0) == level + LEV), 1.0, 0.0)
    u = jnp.dot(winds, spread_u, preferred_element_type=F32, precision=lax.Precision.HIGHEST)
    v = jnp.dot(winds, spread_v, preferred_element_type=F32, precision=lax.Precision.HIGHEST)
    east, west = jnp.maximum(u, 0.0) * q, jnp.minimum(u, 0.0) * q
    north, south = jnp.maximum(v, 0.0) * q, jnp.minimum(v, 0.0) * q
    r8, c8 = iota((ROWS, CELLS), 0), iota((ROWS, CELLS), 1)
    strip_v[0] = dot(onehot(c8 == r8 * COLS), (-west).astype(BF16)).astype(BF16)
    strip_v[1] = dot(onehot(c8 == r8 * COLS + COLS - 1), east.astype(BF16)).astype(BF16)
    for b in (0, 1):
        strip_h[0, b] = (-south[8 * b : 8 * b + 8]).astype(BF16)
        strip_h[1, b] = north[CELLS - 16 + 8 * b : CELLS - 8 + 8 * b].astype(BF16)

    pl.semaphore_wait(barrier, arrivals)

    def copy(source, target, send, recv, dev):
        return pltpu.make_async_remote_copy(
            src_ref=source, dst_ref=target, send_sem=send, recv_sem=recv, device_id=dev, device_id_type=MESH
        )

    for role, r, c, source, target, send, recv in relay:
        @pl.when(jnp.logical_and(role, elsewhere(r, c)))
        def _():
            copy(source, target, send, recv, device(r, c)).start()

        @pl.when(jnp.logical_and(role, jnp.logical_not(elsewhere(r, c))))
        def _():
            pltpu.make_async_copy(source, target, recv).start()

    for condition, dev, source, target, send, recv in halo:
        @pl.when(condition)
        def _():
            copy(source, target, send, recv, dev).start()

    column = iota((CELLS, PAD), 0) % COLS
    zero16 = jnp.zeros((COLS, PAD), F32)
    east_in = jnp.where(column == 0, 0.0, pltpu.roll(east, 1, 0))
    west_in = jnp.where(column == COLS - 1, 0.0, pltpu.roll(west, CELLS - 1, 0))
    north_in = jnp.concatenate([zero16, north[: CELLS - COLS]], axis=0)
    south_in = jnp.concatenate([south[COLS:], zero16], axis=0)
    partial = q - ((east + west_in) - (east_in + west)) - ((north + south_in) - (north_in + south))

    owner_row = owner_ref[...].astype(F32)
    ii, jj = iota((CELLS, CELLS), 0), iota((CELLS, CELLS), 1)
    owner_col = jnp.sum(jnp.where(ii == jj, owner_row, 0.0), axis=1, keepdims=True)
    same = owner_col == owner_row
    rank_col = jnp.sum(jnp.where(jnp.logical_and(same, jj < ii), 1.0, 0.0), axis=1, keepdims=True)
    rank_row = jnp.sum(jnp.where(jnp.logical_and(same, ii < jj), 1.0, 0.0), axis=0, keepdims=True)
    slot_col = owner_col * CAP + rank_col
    slot_row = owner_row * CAP + rank_row
    gather = onehot(iota((SLOTS, CELLS), 0).astype(F32) == slot_row)
    spread = onehot(iota((CELLS, SLOTS), 1).astype(F32) == slot_col)

    def select(edge, length, total):
        pos = iota((length, total), 0)
        cand = iota((length, total), 1)
        parts = []
        for target in range(6):
            source_face, source_edge, rev = (links[target, edge, n] for n in range(3))
            start = (source_edge * 2 + rev) * length + rev * (length - 1)
            start = jnp.where(source_face == face, start, -1000)
            parts.append(onehot(cand == start + (1 - 2 * rev) * pos))
        return jnp.concatenate(parts, axis=0)

    def faces(fwd, rim, send, recv):
        for step in range(1, 6):
            other = face_at(step)
            copy(fwd.at[other], rim.at[face], send.at[step], recv, (group, other, tile)).start()
        pltpu.make_async_copy(fwd.at[face], rim.at[face], recv).start()

    @pl.when(is_v)
    def _():
        pltpu.make_async_copy(cand_v, cand_v, cand_recv.at[0]).wait()
        chosen = dot(select(edge_v, 8, 64), cand_v[...].reshape(64, PAD)).astype(BF16)
        fwd_v[...] = chosen.reshape(6, 8, PAD)
        faces(fwd_v, rim_v, rim_send_v, rim_recv.at[0])

    @pl.when(is_h)
    def _():
        pltpu.make_async_copy(cand_h, cand_h, cand_recv.at[1]).wait()
        chosen = dot(select(2 + edge_h, 16, 128), cand_h[...].reshape(128, PAD)).astype(BF16)
        fwd_h[...] = chosen.reshape(6, 2, 8, PAD)
        faces(fwd_h, rim_h, rim_send_h, rim_recv.at[1])

    for (condition, *_), target, recv in zip(
        halo, (ghost_v.at[0], ghost_v.at[1], ghost_h.at[0], ghost_h.at[1]), (0, 1, 2, 3)
    ):
        @pl.when(condition)
        def _():
            pltpu.make_async_copy(target, target, halo_recv.at[recv]).wait()

    @pl.when(is_v)
    def _():
        pltpu.make_async_copy(rim_v, rim_v, rim_recv.at[0]).wait()
        ghost_v[edge_v] = jnp.sum(rim_v[...].astype(F32), axis=0).astype(BF16)

    @pl.when(is_h)
    def _():
        pltpu.make_async_copy(rim_h, rim_h, rim_recv.at[1]).wait()
        ghost_h[edge_h] = jnp.sum(rim_h[...].astype(F32), axis=0).astype(BF16)

    cell16, pos16 = iota((CELLS, 16), 0), iota((CELLS, 16), 1)
    side = jnp.where(pos16 < 8, pos16 * COLS, (pos16 - 8) * COLS + COLS - 1)
    advected = (
        partial
        + dot(onehot(cell16 == side), ghost_v[...].reshape(16, PAD))
        + dot(onehot(cell16 == pos16), ghost_h[0].reshape(16, PAD))
        + dot(onehot(cell16 == pos16 + CELLS - COLS), ghost_h[1].reshape(16, PAD))
    )
    gap = jnp.zeros((CELLS, FPAD - PAD), F32)
    change = pltpu.roll(jnp.concatenate([advected - q, gap], axis=1), WIDE, 1)
    features = jnp.where(iota((CELLS, FPAD), 1) < WIDE, jnp.concatenate([advected, gap], axis=1), change)
    outbox[...] = dot(gather, features.astype(BF16)).astype(BF16).reshape(TILES, CAP, FPAD)

    def exchange(box, target, send, recv):
        own = pltpu.make_async_copy(box.at[tile], target.at[tile], own_sem)
        own.start()

        def step(i, carry):
            other = owner_at(i)
            copy(box.at[other], target.at[tile], send, recv, (group, face, other)).start()
            return carry

        lax.fori_loop(1, TILES, step, 0)
        own.wait()
        most = target.at[pl.ds(0, TILES - 1)]
        pltpu.make_async_copy(most, most, recv).wait()

    exchange(outbox, inbox, a2a_send, a2a_recv)
    for load in loads:
        load.wait()
    x = inbox[...].reshape(SLOTS, FPAD)[:, :FEAT]
    hidden = silu(dot(x, first[...])).astype(BF16)
    hidden = silu(dot(hidden, middle[...])).astype(BF16)
    reply[:, :, :WIDE] = dot(hidden, last[...]).astype(BF16).reshape(TILES, CAP, WIDE)
    exchange(reply, answers, ret_send, ret_recv)
    tendency = dot(spread, answers[...].reshape(SLOTS, PAD))
    out_ref[...] = (advected + tendency)[:, :WIDE]

    for role, r, c, source, target, send, recv in relay:
        @pl.when(jnp.logical_and(role, elsewhere(r, c)))
        def _():
            copy(source, target, send, recv, device(r, c)).wait_send()
    for condition, dev, source, target, send, recv in halo:
        @pl.when(condition)
        def _():
            copy(source, target, send, recv, dev).wait_send()
    for role, fwd, rim, send in ((is_v, fwd_v, rim_v, rim_send_v), (is_h, fwd_h, rim_h, rim_send_h)):
        @pl.when(role)
        def _():
            for step in range(1, 6):
                other = face_at(step)
                copy(fwd.at[other], rim.at[face], send.at[step], rim_recv.at[0], (group, other, tile)).wait_send()
    most = outbox.at[pl.ds(0, TILES - 1)]
    pltpu.make_async_copy(most, most, a2a_send).wait()
    most = reply.at[pl.ds(0, TILES - 1)]
    pltpu.make_async_copy(most, most, ret_send).wait()


def local(tracers, wind_field, face_links, owner_map, first_layer, middle_layer, last_layer):
    vmem = pl.BlockSpec(memory_space=pltpu.VMEM)
    smem = pl.BlockSpec(memory_space=pltpu.SMEM)
    hbm = pl.BlockSpec(memory_space=pl.ANY)
    dma = pltpu.SemaphoreType.DMA
    updated = pl.pallas_call(
        kernel,
        out_shape=jax.ShapeDtypeStruct((CELLS, WIDE), F32),
        in_specs=[vmem, vmem, smem, vmem, hbm, hbm, hbm],
        out_specs=vmem,
        scratch_shapes=[
            pltpu.VMEM(first_layer.shape[1:], BF16),
            pltpu.VMEM(middle_layer.shape[1:], BF16),
            pltpu.VMEM(last_layer.shape[1:], BF16),
            pltpu.VMEM((2, 8, PAD), BF16),
            pltpu.VMEM((2, 2, 8, PAD), BF16),
            pltpu.VMEM((2, 8, PAD), BF16),
            pltpu.VMEM((2, 2, 8, PAD), BF16),
            pltpu.VMEM((8, 8, PAD), BF16),
            pltpu.VMEM((8, 2, 8, PAD), BF16),
            pltpu.VMEM((6, 8, PAD), BF16),
            pltpu.VMEM((6, 2, 8, PAD), BF16),
            pltpu.VMEM((6, 8, PAD), BF16),
            pltpu.VMEM((6, 2, 8, PAD), BF16),
            pltpu.VMEM((CELLS, PAD), F32),
            pltpu.VMEM((TILES, CAP, FPAD), BF16),
            pltpu.VMEM((TILES, CAP, FPAD), BF16),
            pltpu.VMEM((TILES, CAP, PAD), BF16),
            pltpu.VMEM((TILES, CAP, PAD), BF16),
            dma((3,)),
            dma((4,)),
            dma((4,)),
            dma((20,)),
            dma((2,)),
            dma((6,)),
            dma((6,)),
            dma((2,)),
            dma, dma, dma, dma, dma,
        ],
        compiler_params=pltpu.CompilerParams(collective_id=0, has_side_effects=True),
    )(
        tracers.reshape(CELLS, WIDE),
        wind_field.reshape(CELLS, 2 * LEV),
        face_links,
        owner_map.reshape(1, CELLS),
        first_layer[0],
        middle_layer[0],
        last_layer[0],
    )
    return updated.reshape(tracers.shape)


def solution(mesh):
    in_specs = (
        P("face", ("group", "tile"), None, None, None),
        P("face", ("group", "tile"), None, None, None),
        P(),
        P("face", ("group", "tile"), None, None),
        P("tile", None, None),
        P("tile", None, None),
        P("tile", None, None),
    )
    out_specs = P("face", ("group", "tile"), None, None, None)
    return jax.shard_map(local, mesh=mesh, in_specs=in_specs, out_specs=out_specs, check_vma=False)
```

time: 1190 us -> 79.8 us (0.07)
  the two profiles are of different devices: /device:TPU:6 before, /device:TPU:88 now
where the time goes in v1:
time: 79.8 us; the launch traced here: 79.5 us
  Pallas kernels  74.6 us (93%)
  local copies, waits for them, and re-layouts  4.89 us (6%)
    pallas_call x1, Pallas kernels, local(): pl.pallas_call(kernel, out_shape=jax.ShapeDtypeStruct((CELLS, WIDE), F32)...  74.6 us
    unnamed x5, local copies, waits for them, and re-layouts  4.89 us

profile of v1, /device:TPU:88, one launch (start us, length us, event | category | flops | bytes accessed | tf_op | source)
XLA Modules:
  0.0 79.5 jit_solution(8463359131633446903)
XLA Ops:
  0.0 0.0 copy-start
  0.0 0.7 copy-done
  0.7 0.7 copy.9.links
  1.4 1.9 %copy.8 = bf16[1,512,316]{2,1,0:T(8,128)(2,1)} copy(bf16[1,512,316]{1,2,0:T(8,128)(2,1)} %param.13) | data formatting | bytes 647168 | tf_op args[6]
  3.3 74.6 %shard_map.73 = f32[128,316]{1,0:T(8,128)} custom-call(f32[128,316]{1,0:T(8,128)} %bitcast.11, f32[128,158]{1,0:T(8,128)} %bitcast.12, s32[6,4,3]{2,1,0:T(4,128)} %copy.9.links, s32[1,128]{1,0:T(1,128)} %bitcast.13, bf16[632,512]{1,0:T(8,128)(2,1)} %bitcast.9, bf16[512,512]{1,0:T(8,128)(2,1)} %bitcast.10, bf16[512,316]{1,0:T(8,128)(2,1)} %bitcast.7), custom_call_target="tpu_custom_call" | custom-call | tf_op jit(solution)/shard_map/pallas_call | solution.py:323
  77.9 1.6 %copy.11 = f32[1,1,8,16,316]{4,3,2,1,0:T(8,128)} copy(f32[1,1,8,16,316]{4,3,2,1,0:T(8,128)} %bitcast.8) | data formatting | bytes 323584
Async XLA Ops:
  0.0 0.7 copy-start

commit v2 on v1

--- a/solution.py
+++ b/solution.py
@@ -49,7 +49,7 @@
     cand_v, cand_h, fwd_v, fwd_h, rim_v, rim_h,
     wide, outbox, inbox, reply, answers,
     wsem, halo_send, halo_recv, cand_send, cand_recv, rim_send_v, rim_send_h, rim_recv,
-    a2a_send, a2a_recv, ret_send, ret_recv, own_sem,
+    a2a_send, a2a_recv, ret_send, ret_recv, own_sem, lines,
 ):
     group, face, tile = (lax.axis_index(a) for a in ("group", "face", "tile"))
     row = tile // 4
@@ -123,7 +123,7 @@
     def count(condition):
         return jnp.where(condition, 1, 0)
 
-    arrivals = jnp.int32(TILES - 1)
+    arrivals = jnp.int32(14)
     for condition, dev, *_ in halo:
         pl.when(condition)(functools.partial(signal, dev))
         arrivals += count(condition)
@@ -144,11 +144,9 @@
         z = lax.rem(tile % 2 + i % 2, 2)
         return y * 8 + x * 2 + z
 
-    def signal_owner(i, carry):
+    for i in range(1, 8):
         signal((group, face, owner_at(i)))
-        return carry
-
-    lax.fori_loop(1, TILES, signal_owner, 0)
+        signal((group, face, owner_at(8 * i)))
 
     wide[:, 256:] = jnp.zeros((CELLS, PAD - 256), F32)
     wide[:, :WIDE] = q_ref[...]
@@ -170,6 +168,8 @@
         strip_h[1, b] = north[CELLS - 16 + 8 * b : CELLS - 8 + 8 * b].astype(BF16)
 
     pl.semaphore_wait(barrier, arrivals)
+    for i in range(1, 8):
+        pl.semaphore_signal(lines, inc=1, device_id=(group, face, owner_at(8 * i)), device_id_type=MESH)
 
     def copy(source, target, send, recv, dev):
         return pltpu.make_async_remote_copy(
@@ -214,7 +214,7 @@
         cand = iota((length, total), 1)
         parts = []
         for target in range(6):
-            source_face, source_edge, rev = (links[target, edge, n] for n in range(3))
+            source_face, source_edge, rev = (links[n, edge, target] for n in range(3))
             start = (source_edge * 2 + rev) * length + rev * (length - 1)
             start = jnp.where(source_face == face, start, -1000)
             parts.append(onehot(cand == start + (1 - 2 * rev) * pos))
@@ -284,13 +284,15 @@
         most = target.at[pl.ds(0, TILES - 1)]
         pltpu.make_async_copy(most, most, recv).wait()
 
+    pl.semaphore_wait(lines, 7)
     exchange(outbox, inbox, a2a_send, a2a_recv)
     for load in loads:
         load.wait()
     x = inbox[...].reshape(SLOTS, FPAD)[:, :FEAT]
     hidden = silu(dot(x, first[...])).astype(BF16)
     hidden = silu(dot(hidden, middle[...])).astype(BF16)
-    reply[:, :, :WIDE] = dot(hidden, last[...]).astype(BF16).reshape(TILES, CAP, WIDE)
+    out = lax.dot_general(hidden, last[...], (((1,), (1,)), ((), ())), preferred_element_type=F32)
+    reply[:, :, :WIDE] = out.astype(BF16).reshape(TILES, CAP, WIDE)
     exchange(reply, answers, ret_send, ret_recv)
     tendency = dot(spread, answers[...].reshape(SLOTS, PAD))
     out_ref[...] = (advected + tendency)[:, :WIDE]
@@ -328,7 +330,7 @@
         scratch_shapes=[
             pltpu.VMEM(first_layer.shape[1:], BF16),
             pltpu.VMEM(middle_layer.shape[1:], BF16),
-            pltpu.VMEM(last_layer.shape[1:], BF16),
+            pltpu.VMEM(last_layer.shape[:0:-1], BF16),
             pltpu.VMEM((2, 8, PAD), BF16),
             pltpu.VMEM((2, 2, 8, PAD), BF16),
             pltpu.VMEM((2, 8, PAD), BF16),
@@ -353,16 +355,17 @@
             dma((6,)),
             dma((2,)),
             dma, dma, dma, dma, dma,
+            pltpu.SemaphoreType.REGULAR,
         ],
         compiler_params=pltpu.CompilerParams(collective_id=0, has_side_effects=True),
     )(
         tracers.reshape(CELLS, WIDE),
         wind_field.reshape(CELLS, 2 * LEV),
-        face_links,
+        face_links.transpose(2, 1, 0),
         owner_map.reshape(1, CELLS),
         first_layer[0],
         middle_layer[0],
-        last_layer[0],
+        last_layer[0].T,
     )
     return updated.reshape(tracers.shape)
 

time: 79.8 us -> 69.3 us (0.87)
  the two profiles are of different devices: /device:TPU:88 before, /device:TPU:72 now
where the time goes in v2:
time: 69.3 us; the launch traced here: 69.2 us
  Pallas kernels  67.5 us (97%)
  local copies, waits for them, and re-layouts  1.62 us (2%)
    pallas_call x1, Pallas kernels, local(): pl.pallas_call(kernel, out_shape=jax.ShapeDtypeStruct((CELLS, WIDE), F32)...  67.5 us
    unnamed x1, local copies, waits for them, and re-layouts  1.62 us

profile of v2, /device:TPU:72, one launch (start us, length us, event | category | flops | bytes accessed | tf_op | source)
XLA Modules:
  0.0 69.2 jit_solution(14469997785286648768)
XLA Ops:
  0.0 67.5 %shard_map.73 = f32[128,316]{1,0:T(8,128)} custom-call(f32[128,316]{1,0:T(8,128)} %bitcast.14, f32[128,158]{1,0:T(8,128)} %bitcast.15, s32[3,4,6]{2,1,0:T(4,128)} %bitcast.16, s32[1,128]{1,0:T(1,128)} %bitcast.17, bf16[632,512]{1,0:T(8,128)(2,1)} %bitcast.11, bf16[512,512]{1,0:T(8,128)(2,1)} %bitcast.12, bf16[316,512]{1,0:T(8,128)(2,1)} %bitcast.13), custom_call_target="tpu_custom_call" | custom-call | tf_op jit(solution)/shard_map/pallas_call | solution.py:325
  67.5 1.6 %copy.9 = f32[1,1,8,16,316]{4,3,2,1,0:T(8,128)} copy(f32[1,1,8,16,316]{4,3,2,1,0:T(8,128)} %bitcast.10) | data formatting | bytes 323584

commit v3 on v2

--- a/solution.py
+++ b/solution.py
@@ -49,7 +49,7 @@
     cand_v, cand_h, fwd_v, fwd_h, rim_v, rim_h,
     wide, outbox, inbox, reply, answers,
     wsem, halo_send, halo_recv, cand_send, cand_recv, rim_send_v, rim_send_h, rim_recv,
-    a2a_send, a2a_recv, ret_send, ret_recv, own_sem, lines,
+    a2a_send, a2a_recv, ret_send, ret_recv, lines,
 ):
     group, face, tile = (lax.axis_index(a) for a in ("group", "face", "tile"))
     row = tile // 4
@@ -61,13 +61,12 @@
     edge_v = group
     edge_h = jnp.where(is_n, 1, 0)
 
-    loads = [
-        pltpu.make_async_copy(first_hbm, first, wsem.at[0]),
-        pltpu.make_async_copy(middle_hbm, middle, wsem.at[1]),
-        pltpu.make_async_copy(last_hbm, last, wsem.at[2]),
-    ]
-    for load in loads:
-        load.start()
+    tile_y, tile_x, half = tile // 8, (tile // 2) % 4, tile % 2
+    pair_depth = lax.rem(6 * half + face + jnp.where(face < 3, 9, 3), 12)
+    pair_half, pair_face = pair_depth // 6, pair_depth % 6
+    weights = ((first_hbm, first, 0), (middle_hbm, middle, 1), (last_hbm, last, 2))
+    for source, target, n in weights:
+        pltpu.make_async_copy(source, target, wsem.at[n]).start()
 
     def device(r, c):
         g, k = place_of(c)
@@ -123,7 +122,7 @@
     def count(condition):
         return jnp.where(condition, 1, 0)
 
-    arrivals = jnp.int32(14)
+    arrivals = jnp.int32(0)
     for condition, dev, *_ in halo:
         pl.when(condition)(functools.partial(signal, dev))
         arrivals += count(condition)
@@ -138,15 +137,16 @@
                 signal((group, face_at(step), tile))
         arrivals += 5 * count(role)
 
-    def owner_at(i):
-        y = lax.rem(tile // 8 + i // 8, 8)
-        x = lax.rem((tile // 2) % 4 + (i // 2) % 4, 4)
-        z = lax.rem(tile % 2 + i % 2, 2)
-        return y * 8 + x * 2 + z
-
-    for i in range(1, 8):
-        signal((group, face, owner_at(i)))
-        signal((group, face, owner_at(8 * i)))
+    def at(partner, y, x):
+        f, z = jnp.where(partner == 1, pair_face, face), jnp.where(partner == 1, pair_half, half)
+        return (group, f, lax.rem(tile_y + y, 8) * 8 + lax.rem(tile_x + x, 4) * 2 + z)
+
+    for x in range(1, 4):
+        signal(at(0, 0, x))
+    for y in range(1, 8):
+        signal(at(0, y, 0))
+    signal(at(1, 0, 0))
+    arrivals += 11
 
     wide[:, 256:] = jnp.zeros((CELLS, PAD - 256), F32)
     wide[:, :WIDE] = q_ref[...]
@@ -168,8 +168,8 @@
         strip_h[1, b] = north[CELLS - 16 + 8 * b : CELLS - 8 + 8 * b].astype(BF16)
 
     pl.semaphore_wait(barrier, arrivals)
-    for i in range(1, 8):
-        pl.semaphore_signal(lines, inc=1, device_id=(group, face, owner_at(8 * i)), device_id_type=MESH)
+    for x in range(1, 4):
+        pl.semaphore_signal(lines.at[0], inc=1, device_id=at(0, 0, x), device_id_type=MESH)
 
     def copy(source, target, send, recv, dev):
         return pltpu.make_async_remote_copy(
@@ -208,6 +208,10 @@
     slot_row = owner_row * CAP + rank_row
     gather = onehot(iota((SLOTS, CELLS), 0).astype(F32) == slot_row)
     spread = onehot(iota((CELLS, SLOTS), 1).astype(F32) == slot_col)
+
+    pl.semaphore_wait(lines.at[0], 3)
+    for y in range(1, 8):
+        pl.semaphore_signal(lines.at[1], inc=1, device_id=at(0, y, 0), device_id_type=MESH)
 
     def select(edge, length, total):
         pos = iota((length, total), 0)
@@ -270,30 +274,39 @@
     features = jnp.where(iota((CELLS, FPAD), 1) < WIDE, jnp.concatenate([advected, gap], axis=1), change)
     outbox[...] = dot(gather, features.astype(BF16)).astype(BF16).reshape(TILES, CAP, FPAD)
 
-    def exchange(box, target, send, recv):
-        own = pltpu.make_async_copy(box.at[tile], target.at[tile], own_sem)
-        own.start()
+    chip = tile_y * 4 + tile_x
+    pl.semaphore_wait(lines.at[1], 7)
+
+    def exchange(box, target, box_index, target_index, send, recv):
+        def remote(y, x, partner):
+            dev = at(partner, y, x)
+            there = dev[2] // 2
+            return copy(box.at[box_index(there, partner)], target.at[target_index(partner)], send, recv, dev)
 
         def step(i, carry):
-            other = owner_at(i)
-            copy(box.at[other], target.at[tile], send, recv, (group, face, other)).start()
+            remote(1 + i // 8, (i // 2) % 4, 1 - i % 2).start()
             return carry
 
-        lax.fori_loop(1, TILES, step, 0)
-        own.wait()
-        most = target.at[pl.ds(0, TILES - 1)]
-        pltpu.make_async_copy(most, most, recv).wait()
-
-    pl.semaphore_wait(lines, 7)
-    exchange(outbox, inbox, a2a_send, a2a_recv)
-    for load in loads:
-        load.wait()
+        lax.fori_loop(0, 57, step, 0)
+        lax.fori_loop(58, TILES, step, 0)
+        pltpu.make_async_copy(box.at[box_index(chip, 0)], target.at[target_index(0)], recv).start()
+        pltpu.make_async_copy(target, target, recv).wait()
+
+    def expert(there, partner):
+        return there * 2 + jnp.where(partner == 1, 1 - half, half)
+
+    def block(there, partner):
+        return partner * 32 + there
+
+    exchange(outbox, inbox, expert, lambda partner: block(chip, partner), a2a_send, a2a_recv)
+    for source, target, n in weights:
+        pltpu.make_async_copy(source, target, wsem.at[n]).wait()
     x = inbox[...].reshape(SLOTS, FPAD)[:, :FEAT]
     hidden = silu(dot(x, first[...])).astype(BF16)
     hidden = silu(dot(hidden, middle[...])).astype(BF16)
     out = lax.dot_general(hidden, last[...], (((1,), (1,)), ((), ())), preferred_element_type=F32)
     reply[:, :, :WIDE] = out.astype(BF16).reshape(TILES, CAP, WIDE)
-    exchange(reply, answers, ret_send, ret_recv)
+    exchange(reply, answers, block, lambda partner: expert(chip, 0), ret_send, ret_recv)
     tendency = dot(spread, answers[...].reshape(SLOTS, PAD))
     out_ref[...] = (advected + tendency)[:, :WIDE]
 
@@ -311,10 +324,9 @@
             for step in range(1, 6):
                 other = face_at(step)
                 copy(fwd.at[other], rim.at[face], send.at[step], rim_recv.at[0], (group, other, tile)).wait_send()
-    most = outbox.at[pl.ds(0, TILES - 1)]
-    pltpu.make_async_copy(most, most, a2a_send).wait()
-    most = reply.at[pl.ds(0, TILES - 1)]
-    pltpu.make_async_copy(most, most, ret_send).wait()
+    for box, send in ((outbox, a2a_send), (reply, ret_send)):
+        most = box.at[pl.ds(0, TILES - 1)]
+        pltpu.make_async_copy(most, most, send).wait()
 
 
 def local(tracers, wind_field, face_links, owner_map, first_layer, middle_layer, last_layer):
@@ -354,8 +366,8 @@
             dma((6,)),
             dma((6,)),
             dma((2,)),
-            dma, dma, dma, dma, dma,
-            pltpu.SemaphoreType.REGULAR,
+            dma, dma, dma, dma,
+            pltpu.SemaphoreType.REGULAR((2,)),
         ],
         compiler_params=pltpu.CompilerParams(collective_id=0, has_side_effects=True),
     )(

time: 69.3 us -> 63.5 us (0.916)
  the two profiles are of different devices: /device:TPU:72 before, /device:TPU:6 now
where the time goes in v3:
time: 63.5 us; the launch traced here: 63.1 us
  Pallas kernels  61.4 us (97%)
  local copies, waits for them, and re-layouts  1.62 us (3%)
    pallas_call x1, Pallas kernels, local(): pl.pallas_call(kernel, out_shape=jax.ShapeDtypeStruct((CELLS, WIDE), F32)...  61.4 us
    unnamed x1, local copies, waits for them, and re-layouts  1.62 us

profile of v3, /device:TPU:6, one launch (start us, length us, event | category | flops | bytes accessed | tf_op | source)
XLA Modules:
  0.0 63.1 jit_solution(18345263024877030998)
XLA Ops:
  0.0 61.4 %shard_map.73 = f32[128,316]{1,0:T(8,128)} custom-call(f32[128,316]{1,0:T(8,128)} %bitcast.14, f32[128,158]{1,0:T(8,128)} %bitcast.15, s32[3,4,6]{2,1,0:T(4,128)} %bitcast.16, s32[1,128]{1,0:T(1,128)} %bitcast.17, bf16[632,512]{1,0:T(8,128)(2,1)} %bitcast.11, bf16[512,512]{1,0:T(8,128)(2,1)} %bitcast.12, bf16[316,512]{1,0:T(8,128)(2,1)} %bitcast.13), custom_call_target="tpu_custom_call" | custom-call | tf_op jit(solution)/shard_map/pallas_call | solution.py:337
  61.4 1.6 %copy.9 = f32[1,1,8,16,316]{4,3,2,1,0:T(8,128)} copy(f32[1,1,8,16,316]{4,3,2,1,0:T(8,128)} %bitcast.10) | data formatting | bytes 323584

commit v4 on v3

--- a/solution.py
+++ b/solution.py
@@ -47,7 +47,7 @@
     first, middle, last,
     strip_v, strip_h, ghost_v, ghost_h,
     cand_v, cand_h, fwd_v, fwd_h, rim_v, rim_h,
-    wide, outbox, inbox, reply, answers,
+    wide, spread_winds, outbox, inbox, reply, answers,
     wsem, halo_send, halo_recv, cand_send, cand_recv, rim_send_v, rim_send_h, rim_recv,
     a2a_send, a2a_recv, ret_send, ret_recv, lines,
 ):
@@ -151,13 +151,19 @@
     wide[:, 256:] = jnp.zeros((CELLS, PAD - 256), F32)
     wide[:, :WIDE] = q_ref[...]
     q = wide[...]
-    winds = w_ref[...]
-    level = lax.rem(iota((2 * LEV, PAD), 1), LEV)
-    inside = iota((2 * LEV, PAD), 1) < WIDE
-    spread_u = jnp.where(jnp.logical_and(inside, iota((2 * LEV, PAD), 0) == level), 1.0, 0.0)
-    spread_v = jnp.where(jnp.logical_and(inside, iota((2 * LEV, PAD), 0) == level + LEV), 1.0, 0.0)
-    u = jnp.dot(winds, spread_u, preferred_element_type=F32, precision=lax.Precision.HIGHEST)
-    v = jnp.dot(winds, spread_v, preferred_element_type=F32, precision=lax.Precision.HIGHEST)
+    spread_winds[:, 2 * LEV :] = jnp.zeros((CELLS, PAD - 2 * LEV), F32)
+    spread_winds[:, : 2 * LEV] = w_ref[...]
+    winds = spread_winds[...]
+    turned = [pltpu.roll(winds, (n * LEV) % PAD, 1) for n in (-1, 0, 1, 2, 3)]
+    lane = iota((CELLS, PAD), 1)
+
+    def repeat(first_turn):
+        value = jnp.where(lane < WIDE, turned[first_turn + 3], 0.0)
+        for n in (2, 1, 0):
+            value = jnp.where(lane < (n + 1) * LEV, turned[first_turn + n], value)
+        return value
+
+    u, v = repeat(1), repeat(0)
     east, west = jnp.maximum(u, 0.0) * q, jnp.minimum(u, 0.0) * q
     north, south = jnp.maximum(v, 0.0) * q, jnp.minimum(v, 0.0) * q
     r8, c8 = iota((ROWS, CELLS), 0), iota((ROWS, CELLS), 1)
@@ -209,10 +215,6 @@
     gather = onehot(iota((SLOTS, CELLS), 0).astype(F32) == slot_row)
     spread = onehot(iota((CELLS, SLOTS), 1).astype(F32) == slot_col)
 
-    pl.semaphore_wait(lines.at[0], 3)
-    for y in range(1, 8):
-        pl.semaphore_signal(lines.at[1], inc=1, device_id=at(0, y, 0), device_id_type=MESH)
-
     def select(edge, length, total):
         pos = iota((length, total), 0)
         cand = iota((length, total), 1)
@@ -243,6 +245,10 @@
         chosen = dot(select(2 + edge_h, 16, 128), cand_h[...].reshape(128, PAD)).astype(BF16)
         fwd_h[...] = chosen.reshape(6, 2, 8, PAD)
         faces(fwd_h, rim_h, rim_send_h, rim_recv.at[1])
+
+    pl.semaphore_wait(lines.at[0], 3)
+    for y in range(1, 8):
+        pl.semaphore_signal(lines.at[1], inc=1, device_id=at(0, y, 0), device_id_type=MESH)
 
     for (condition, *_), target, recv in zip(
         halo, (ghost_v.at[0], ghost_v.at[1], ghost_h.at[0], ghost_h.at[1]), (0, 1, 2, 3)
@@ -277,7 +283,7 @@
     chip = tile_y * 4 + tile_x
     pl.semaphore_wait(lines.at[1], 7)
 
-    def exchange(box, target, box_index, target_index, send, recv):
+    def exchange(box, target, box_index, target_index, send, recv, meanwhile):
         def remote(y, x, partner):
             dev = at(partner, y, x)
             there = dev[2] // 2
@@ -290,6 +296,7 @@
         lax.fori_loop(0, 57, step, 0)
         lax.fori_loop(58, TILES, step, 0)
         pltpu.make_async_copy(box.at[box_index(chip, 0)], target.at[target_index(0)], recv).start()
+        meanwhile()
         pltpu.make_async_copy(target, target, recv).wait()
 
     def expert(there, partner):
@@ -298,35 +305,41 @@
     def block(there, partner):
         return partner * 32 + there
 
-    exchange(outbox, inbox, expert, lambda partner: block(chip, partner), a2a_send, a2a_recv)
-    for source, target, n in weights:
-        pltpu.make_async_copy(source, target, wsem.at[n]).wait()
+    def sent(box, send):
+        most = box.at[pl.ds(0, TILES - 1)]
+        pltpu.make_async_copy(most, most, send).wait()
+
+    def drain():
+        for role, r, c, source, target, send, recv in relay:
+            @pl.when(jnp.logical_and(role, elsewhere(r, c)))
+            def _():
+                copy(source, target, send, recv, device(r, c)).wait_send()
+        for condition, dev, source, target, send, recv in halo:
+            @pl.when(condition)
+            def _():
+                copy(source, target, send, recv, dev).wait_send()
+        for role, fwd, rim, send in ((is_v, fwd_v, rim_v, rim_send_v), (is_h, fwd_h, rim_h, rim_send_h)):
+            @pl.when(role)
+            def _():
+                for step in range(1, 6):
+                    other = face_at(step)
+                    copy(fwd.at[other], rim.at[face], send.at[step], rim_recv.at[0], (group, other, tile)).wait_send()
+        for source, target, n in weights:
+            pltpu.make_async_copy(source, target, wsem.at[n]).wait()
+
+    exchange(outbox, inbox, expert, lambda partner: block(chip, partner), a2a_send, a2a_recv, drain)
     x = inbox[...].reshape(SLOTS, FPAD)[:, :FEAT]
     hidden = silu(dot(x, first[...])).astype(BF16)
     hidden = silu(dot(hidden, middle[...])).astype(BF16)
     out = lax.dot_general(hidden, last[...], (((1,), (1,)), ((), ())), preferred_element_type=F32)
     reply[:, :, :WIDE] = out.astype(BF16).reshape(TILES, CAP, WIDE)
-    exchange(reply, answers, block, lambda partner: expert(chip, 0), ret_send, ret_recv)
+    exchange(
+        reply, answers, block, lambda partner: expert(chip, 0), ret_send, ret_recv, lambda: sent(outbox, a2a_send)
+    )
     tendency = dot(spread, answers[...].reshape(SLOTS, PAD))
     out_ref[...] = (advected + tendency)[:, :WIDE]
 
-    for role, r, c, source, target, send, recv in relay:
-        @pl.when(jnp.logical_and(role, elsewhere(r, c)))
-        def _():
-            copy(source, target, send, recv, device(r, c)).wait_send()
-    for condition, dev, source, target, send, recv in halo:
-        @pl.when(condition)
-        def _():
-            copy(source, target, send, recv, dev).wait_send()
-    for role, fwd, rim, send in ((is_v, fwd_v, rim_v, rim_send_v), (is_h, fwd_h, rim_h, rim_send_h)):
-        @pl.when(role)
-        def _():
-            for step in range(1, 6):
-                other = face_at(step)
-                copy(fwd.at[other], rim.at[face], send.at[step], rim_recv.at[0], (group, other, tile)).wait_send()
-    for box, send in ((outbox, a2a_send), (reply, ret_send)):
-        most = box.at[pl.ds(0, TILES - 1)]
-        pltpu.make_async_copy(most, most, send).wait()
+    sent(reply, ret_send)
 
 
 def local(tracers, wind_field, face_links, owner_map, first_layer, middle_layer, last_layer):
@@ -353,6 +366,7 @@
             pltpu.VMEM((6, 2, 8, PAD), BF16),
             pltpu.VMEM((6, 8, PAD), BF16),
             pltpu.VMEM((6, 2, 8, PAD), BF16),
+            pltpu.VMEM((CELLS, PAD), F32),
             pltpu.VMEM((CELLS, PAD), F32),
             pltpu.VMEM((TILES, CAP, FPAD), BF16),
             pltpu.VMEM((TILES, CAP, FPAD), BF16),

time: 63.5 us -> 63.1 us (level)
  no operation moved by 1% of the time
where the time goes in v4:
time: 63.1 us; the launch traced here: 62.8 us
  Pallas kernels  61.2 us (97%)
  local copies, waits for them, and re-layouts  1.62 us (3%)
    pallas_call x1, Pallas kernels, local(): pl.pallas_call(kernel, out_shape=jax.ShapeDtypeStruct((CELLS, WIDE), F32)...  61.2 us
    unnamed x1, local copies, waits for them, and re-layouts  1.62 us

profile of v4, /device:TPU:6, one launch (start us, length us, event | category | flops | bytes accessed | tf_op | source)
XLA Modules:
  0.0 62.8 jit_solution(17013691148863153449)
XLA Ops:
  0.0 61.2 %shard_map.73 = f32[128,316]{1,0:T(8,128)} custom-call(f32[128,316]{1,0:T(8,128)} %bitcast.14, f32[128,158]{1,0:T(8,128)} %bitcast.15, s32[3,4,6]{2,1,0:T(4,128)} %bitcast.16, s32[1,128]{1,0:T(1,128)} %bitcast.17, bf16[632,512]{1,0:T(8,128)(2,1)} %bitcast.11, bf16[512,512]{1,0:T(8,128)(2,1)} %bitcast.12, bf16[316,512]{1,0:T(8,128)(2,1)} %bitcast.13), custom_call_target="tpu_custom_call" | custom-call | tf_op jit(solution)/shard_map/pallas_call | solution.py:350
  61.2 1.6 %copy.9 = f32[1,1,8,16,316]{4,3,2,1,0:T(8,128)} copy(f32[1,1,8,16,316]{4,3,2,1,0:T(8,128)} %bitcast.10) | data formatting | bytes 323584
